TPU v7x, 32 devices: a whole 2x2x4 slice. The times are simulated.
32 devices in a mesh: row: 4 (over x, core), col: 8 (over z, y).
Axes of the slice: x: 2, y: 2, z: 4, core: 2. Of those that a mesh axis runs over, the one named last changes fastest.
Arguments:
- orbitals: float32 [128, 32, 1024], P(('row', 'col')), may hold values from -6 to 6
- gradient: float32 [128, 32, 1024], P(('row', 'col')), may hold values from -4 to 4
- offsets: int32 [128, 3], replicated, may hold values from 0 to 3
- pairs: int32 [32, 4, 2], P('row'), may hold values from 0 to 127, as said below
- counts: int32 [32], P('row'), may hold values from 1 to 4, as said below
Outputs:
- updated: float32 [128, 32, 1024], P(('row', 'col'))
- energies: float32 [2], replicated
Inputs may be any that keep to these rules, and one draw needn't show every extreme that they name: `pairs`: both orbitals of a slot of pair owner p belong to p's group, ids g * 32 to (g + 1) * 32 - 1 with g = p // 8 (device d owns ids d * 4 onward). Among the live slots of one pair owner at most 2 distinct orbitals come from any one device, and every owner reaches 2 from some device. `counts`: every group of 8 pair owners has one owner with 4 live slots.
All inputs are finite; a program needn't handle non-finite values.
Results may differ from a plain program's by a relative error of at most 0.0082.
Values may be sent and summed in bfloat16 or wider, within the bound.
No kernel may reach another device: no remote copies, remote signals or barrier semaphores. Data moves between devices by JAX's collectives and lax.ppermute only.
A program may use at most 64 MiB of HBM per device.

v0:
```python
import jax
import jax.numpy as jnp
from jax import lax
from jax.sharding import PartitionSpec as P

CAP = 2
SHIFT = 4
SWEEPS = 12
ROUNDS = 2
screen_mu = 0.1
damping = 0.5


def sweep_table(sweeps):
    center_val = 6.0 + screen_mu
    half_width = 6.0
    ratio_val = center_val / half_width
    prev_coef = 1.0 / ratio_val
    keep_list = []
    mix_list = []
    for sweep_idx in range(sweeps):
        next_coef = 1.0 / (2.0 * ratio_val - prev_coef)
        keep_list.append(next_coef * prev_coef)
        mix_list.append(2.0 * next_coef / half_width)
        prev_coef = next_coef
    return (jnp.array(keep_list, jnp.float32), jnp.array(mix_list, jnp.float32), 1.0 / center_val)


def apply_operator(field):
    edge = field.shape[0]
    plane = field.shape[1]
    zero_row = jnp.zeros_like(field[:1])
    along_x = jnp.concatenate([field[1:], zero_row], 0) + jnp.concatenate([zero_row, field[:-1]], 0)
    zero_band = jnp.zeros_like(field[:, :edge])
    along_y = jnp.concatenate([field[:, edge:], zero_band], 1) + jnp.concatenate(
        [zero_band, field[:, :-edge]], 1
    )
    zero_col = jnp.zeros_like(field[:, :1])
    depth = jnp.arange(plane) % edge
    upper = jnp.where(depth < edge - 1, jnp.concatenate([field[:, 1:], zero_col], 1), 0.0)
    lower = jnp.where(depth > 0, jnp.concatenate([zero_col, field[:, :-1]], 1), 0.0)
    return (6.0 + screen_mu) * field - (along_x + along_y + upper + lower)


def screened_solve(source, tables):
    keep_coef, mix_coef, first_coef = tables

    def sweep(index, state):
        solution, remainder, direction = state
        solution = solution + direction
        remainder = remainder - apply_operator(direction)
        direction = keep_coef[index] * direction + mix_coef[index] * remainder
        return (solution, remainder, direction)

    state = (jnp.zeros_like(source), source, source * first_coef)
    return lax.fori_loop(0, keep_coef.shape[0], sweep, state)[0]


def displaced(box, shift):
    edge = box.shape[0]
    reach = SHIFT - 1
    cube = jnp.pad(box.reshape(edge, edge, edge), reach)
    start = shift + reach
    moved = lax.dynamic_slice(cube, (start[0], start[1], start[2]), (edge, edge, edge))
    return moved.reshape(edge, edge * edge)


def run_pairs(boxes, source_of, slot_of, mine, mine_count, group_offsets, tables, slots):
    edge = boxes.shape[1]
    plane = boxes.shape[2]
    collected = jnp.zeros((slots, edge, plane), jnp.float32)

    def one_pair(index, state):
        gathered, energy = state
        first = mine[index, 0]
        second = mine[index, 1]
        shift = group_offsets[first] - group_offsets[second]
        box_i = lax.dynamic_index_in_dim(boxes, source_of[first], 0, False).astype(jnp.float32)
        box_j = displaced(
            lax.dynamic_index_in_dim(boxes, source_of[second], 0, False), shift
        ).astype(jnp.float32)
        density = box_i * box_j
        potential = screened_solve(density, tables)
        term = potential * box_j
        target = slot_of[first]
        current = lax.dynamic_index_in_dim(gathered, target, 0, False)
        gathered = lax.dynamic_update_index_in_dim(gathered, current + term, target, 0)
        return (gathered, energy + jnp.sum(density * potential))

    return lax.fori_loop(0, mine_count, one_pair, (collected, jnp.zeros((), jnp.float32)))


def local(orbitals, gradient, offsets, pairs, counts):
    tables = sweep_table(SWEEPS)
    own_count = orbitals.shape[0]
    edge = orbitals.shape[1]
    plane = orbitals.shape[2]
    columns = lax.axis_size("col")
    own_index = lax.axis_index("col")
    group = columns * own_count
    slots = columns * CAP
    base = lax.axis_index("row") * group
    local_pairs = pairs - base
    group_offsets = lax.dynamic_slice_in_dim(offsets, base, group, 0)
    orbit_ids = jnp.arange(group, dtype=jnp.int32)
    live = jnp.arange(local_pairs.shape[1])[None, :] < counts[:, None]
    hits = (local_pairs[:, :, 0, None] == orbit_ids) | (local_pairs[:, :, 1, None] == orbit_ids)
    needed = (
        jnp.any(hits & live[:, :, None], axis=1)
        .astype(jnp.int32)
        .reshape(columns, columns, own_count)
    )
    ranks = jnp.cumsum(needed, axis=2) - 1
    send_need = lax.dynamic_index_in_dim(needed, own_index, 1, False)
    send_rank = lax.dynamic_index_in_dim(ranks, own_index, 1, False)
    slot_ids = jnp.arange(CAP)
    plan = (
        (send_need[:, None, :] == 1) & (send_rank[:, None, :] == slot_ids[None, :, None])
    ).astype(jnp.bfloat16)
    recv_rank = lax.dynamic_index_in_dim(ranks, own_index, 0, False)
    slot_of = (jnp.arange(columns)[:, None] * CAP + recv_rank).reshape(group)
    mine = lax.dynamic_index_in_dim(local_pairs, own_index, 0, False)
    mine_count = lax.dynamic_index_in_dim(counts, own_index, 0, False)
    current = orbitals
    totals = []
    for round_idx in range(ROUNDS):
        boxes_own = current.astype(jnp.bfloat16)
        outgoing = jnp.einsum(
            "pkm,mc->pkc",
            plan,
            boxes_own.reshape(own_count, edge * plane),
            preferred_element_type=jnp.float32,
        ).astype(jnp.bfloat16)
        arrived = lax.all_to_all(outgoing, "col", split_axis=0, concat_axis=0, tiled=True).reshape(
            slots, edge, plane
        )
        gathered, energy = run_pairs(
            arrived, slot_of, slot_of, mine, mine_count, group_offsets, tables, slots
        )
        slot_terms = gathered.astype(jnp.bfloat16).reshape(columns, CAP, edge * plane)
        returned = lax.all_to_all(slot_terms, "col", split_axis=0, concat_axis=0, tiled=True)
        exchange_term = jnp.einsum(
            "pkm,pkc->mc", plan, returned, preferred_element_type=jnp.float32
        )
        current = current - damping * (gradient + exchange_term.reshape(own_count, edge, plane))
        totals.append(energy)
    summed = lax.psum(jnp.stack(totals), ("row", "col"))
    energies = summed / (edge * edge * edge * lax.axis_size("row") * columns)
    return (current, energies)


def solution(mesh):
    return jax.shard_map(
        local,
        mesh=mesh,
        in_specs=(
            P(("row", "col"), None, None),
            P(("row", "col"), None, None),
            P(),
            P("row", None, None),
            P("row"),
        ),
        out_specs=(P(("row", "col"), None, None), P()),
        check_vma=False,
    )
```

profile of v0, /device:TPU:0, one launch (start us, length us, event | category | flops | bytes accessed | tf_op | source)
XLA Modules:
  0.0 598.3 jit_solution(14379024483895051703)
XLA Ops:
  4.1 2.1 copy.30
  6.1 7.3 %all-to-all-start = ((bf16[8,2,32768]{2,1,0:T(2,128)(2,1)}), bf16[8,2,32768]{2,1,0:T(2,128)(2,1)S(1)}, u32[]{:S(2)}, u32[]{:S(2)}) async-start(bf16[8,2,32768]{2,1,0:T(2,128)(2,1)} %copy.30), calls=%async_computation | async-start | bytes 2097152 | tf_op jit(solution)/shard_map/all_to_all | solution.py:134
  14.8 24.4 %all-to-all-done = bf16[8,2,32768]{2,1,0:T(2,128)(2,1)S(1)} async-done(((bf16[8,2,32768]{2,1,0:T(2,128)(2,1)}), bf16[8,2,32768]{2,1,0:T(2,128)(2,1)S(1)}, u32[]{:S(2)}, u32[]{:S(2)}) %all-to-all-start) | async-done | bytes 1048608 | tf_op jit(solution)/shard_map/all_to_all | solution.py:134
  39.2 1.6 reshape.110
  41.1 54.8 %while.91 = (s32[]{:T(128)}, f32[16,32,1024]{2,1,0:T(8,128)S(1)}, f32[]{:T(128)}, s32[]{:T(128)}, s32[4,2]{0,1:T(2,128)S(1)}, /*index=5*/s32[32]{0:T(128)S(1)}, ...) while((s32[]{:T(128)}, f32[16,32,1024]{2,1,0:T(8,128)S(1)}, ...), condition=%wide.region_6.7_spmd.clone, body=%wide.region_2.6_spmd.sunk.clone.sunk | while | flops 761891 | bytes 5591096 | solution.py:90
  59.2 34.8 %while.94 = (s32[]{:T(128)}, f32[32,1024]{1,0:T(8,128)S(1)}, f32[32,1024]{1,0:T(8,128)S(1)}, f32[32,1024]{1,0:T(8,128)S(1)}, s32[]{:T(128)}, /*index=5*/f32[12]{0:T(128)S(1)}, f32[12]{0:T(128)S(1)}, s32[]{:T(128)}) while((s32[]{:T(128)}, f32[32,1024]{1,0:T(8,128)S(1)}, f32[32,1024]{1,0:T(8,128)S(1)}, ...), condition=%wide.region_4.4_spmd.clone.clone, body=%wide.region_3.3_spmd.sunk.clone.clone.sunk | while | flops 499715 | bytes 3100039 | solution.py:56
  60.7 1.4 multiply_add_fusion.5
  63.6 1.4 multiply_add_fusion.5
  66.5 1.4 multiply_add_fusion.5
  69.4 1.4 multiply_add_fusion.5
  72.3 1.4 multiply_add_fusion.5
  75.2 1.4 multiply_add_fusion.5
  78.0 1.4 multiply_add_fusion.5
  96.9 189.4 %all_to_all.20 = bf16[8,2,32768]{2,1,0:T(2,128)(2,1)S(1)} all-to-all(bf16[8,2,32768]{2,1,0:T(2,128)(2,1)S(1)} %reshape.111), channel_id=1, replica_groups=mesh['row'=4,'col'=8] {'col'}, dimensions={0} | all-to-all | bytes 2097152 | tf_op jit(solution)/shard_map/all_to_all | solution.py:141
  288.8 2.1 copy.32
  290.9 3.6 all-to-all-start.2
  294.5 25.6 %all-to-all-done.2 = bf16[8,2,32768]{2,1,0:T(2,128)(2,1)S(1)} async-done(((bf16[8,2,32768]{2,1,0:T(2,128)(2,1)}), bf16[8,2,32768]{2,1,0:T(2,128)(2,1)S(1)}, u32[]{:S(2)}, u32[]{:S(2)}) %all-to-all-start.2) | async-done | bytes 1048608 | tf_op jit(solution)/shard_map/all_to_all | solution.py:134
  320.1 1.6 reshape.114
  322.0 55.1 %while.93 = (s32[]{:T(128)}, f32[16,32,1024]{2,1,0:T(8,128)S(1)}, f32[]{:T(128)}, s32[]{:T(128)}, s32[4,2]{0,1:T(2,128)S(1)}, /*index=5*/s32[32]{0:T(128)S(1)}, ...) while((s32[]{:T(128)}, f32[16,32,1024]{2,1,0:T(8,128)S(1)}, ...), condition=%wide.region_11.12_spmd.clone, body=%wide.region_7.11_spmd.sunk.clone.sunk | while | flops 761891 | bytes 5591080 | solution.py:90
  340.0 35.1 %while.95 = (s32[]{:T(128)}, f32[32,1024]{1,0:T(8,128)S(1)}, f32[32,1024]{1,0:T(8,128)S(1)}, f32[32,1024]{1,0:T(8,128)S(1)}, s32[]{:T(128)}, /*index=5*/f32[12]{0:T(128)S(1)}, f32[12]{0:T(128)S(1)}, s32[]{:T(128)}) while((s32[]{:T(128)}, f32[32,1024]{1,0:T(8,128)S(1)}, f32[32,1024]{1,0:T(8,128)S(1)}, ...), condition=%wide.region_9.9_spmd.clone.clone, body=%wide.region_8.8_spmd.sunk.clone.clone.sunk | while | flops 499715 | bytes 3100039 | solution.py:56
  377.2 1.6 reshape.115
  378.8 164.4 %all-to-all-start.3 = ((bf16[8,2,32768]{2,1,0:T(2,128)(2,1)}), bf16[8,2,32768]{2,1,0:T(2,128)(2,1)S(1)}, u32[]{:S(2)}, u32[]{:S(2)}) async-start(bf16[8,2,32768]{2,1,0:T(2,128)(2,1)} %reshape.115), calls=%async_computation.3 | async-start | bytes 2097152 | tf_op jit(solution)/shard_map/all_to_all | solution.py:141
  543.3 52.2 %psum.7 = f32[2]{0:T(128)S(1)} all-reduce(f32[2]{0:T(128)S(1)} %pad_maximum_fusion), channel_id=1, replica_groups=mesh['row'=4,'col'=8] {'row','col'}, use_global_device_ids=true, to_apply=%region_12.13 | all-reduce | flops 2 | bytes 16 | tf_op jit(solution)/shard_map/psum | solution.py:147
  596.8 1.5 fusion.17
  (246 shorter events, 79.0 us)
Async XLA Ops:
  0.6 14.1 %copy-start = (s32[128,3]{0,1:T(4,128)S(1)}, s32[128,3]{0,1:T(4,128)}, u32[]{:S(2)}) copy-start(s32[128,3]{0,1:T(4,128)} %param.17) | copy-start | bytes 4612
  4.1 9.4 %copy-start.7 = (s32[8]{0:T(128)S(1)}, s32[8]{0:T(128)}, u32[]{:S(2)}) copy-start(s32[8]{0:T(128)} %param.19) | copy-start | bytes 100
  6.1 33.1 %all-to-all-start = ((bf16[8,2,32768]{2,1,0:T(2,128)(2,1)}), bf16[8,2,32768]{2,1,0:T(2,128)(2,1)S(1)}, u32[]{:S(2)}, u32[]{:S(2)}) async-start(bf16[8,2,32768]{2,1,0:T(2,128)(2,1)} %copy.30), calls=%async_computation | async-start | bytes 2097152 | tf_op jit(solution)/shard_map/all_to_all | solution.py:134
  14.8 26.2 %copy-start.8 = (f32[12]{0:T(128)S(1)}, f32[12]{0:T(128)}, u32[]{:S(2)}) copy-start(f32[12]{0:T(128)} %constant.362.clone..sunk2.5) | copy-start | bytes 148
  14.8 26.3 %copy-start.9 = (f32[12]{0:T(128)S(1)}, f32[12]{0:T(128)}, u32[]{:S(2)}) copy-start(f32[12]{0:T(128)} %constant.363.clone..sunk2.5) | copy-start | bytes 148
  96.8 190.9 %copy-start.1 = (f32[4,32,1024]{2,1,0:T(8,128)S(1)}, f32[4,32,1024]{2,1,0:T(8,128)}, u32[]{:S(2)}) copy-start(f32[4,32,1024]{2,1,0:T(8,128)} %param.15) | copy-start | bytes 1572868
  96.9 190.9 %copy-start.5 = (f32[4,32,1024]{2,1,0:T(8,128)S(1)}, f32[4,32,1024]{2,1,0:T(8,128)}, u32[]{:S(2)}) copy-start(f32[4,32,1024]{2,1,0:T(8,128)} %param.16) | copy-start | bytes 1572868
  287.0 0.8 copy-start.3
  290.9 29.2 %all-to-all-start.2 = ((bf16[8,2,32768]{2,1,0:T(2,128)(2,1)}), bf16[8,2,32768]{2,1,0:T(2,128)(2,1)S(1)}, u32[]{:S(2)}, u32[]{:S(2)}) async-start(bf16[8,2,32768]{2,1,0:T(2,128)(2,1)} %copy.32), calls=%async_computation.2 | async-start | bytes 2097152 | tf_op jit(solution)/shard_map/all_to_all | solution.py:134
  378.8 218.0 %copy-start.2 = (f32[4,32,1024]{2,1,0:T(8,128)S(1)}, f32[4,32,1024]{2,1,0:T(8,128)}, u32[]{:S(2)}) copy-start(f32[4,32,1024]{2,1,0:T(8,128)} %param.15) | copy-start | bytes 1572868
  378.8 218.0 %copy-start.4 = (f32[4,32768,1]{1,0,2:T(4,128)S(1)}, f32[4,32768,1]{1,0,2:T(4,128)}, u32[]{:S(2)}) copy-start(f32[4,32768,1]{1,0,2:T(4,128)} %copy-done.3) | copy-start | bytes 1572868
  378.8 218.0 %copy-start.6 = (f32[4,32,1024]{2,1,0:T(8,128)S(1)}, f32[4,32,1024]{2,1,0:T(8,128)}, u32[]{:S(2)}) copy-start(f32[4,32,1024]{2,1,0:T(8,128)} %param.16) | copy-start | bytes 1572868
  378.8 217.3 %all-to-all-start.3 = ((bf16[8,2,32768]{2,1,0:T(2,128)(2,1)}), bf16[8,2,32768]{2,1,0:T(2,128)(2,1)S(1)}, u32[]{:S(2)}, u32[]{:S(2)}) async-start(bf16[8,2,32768]{2,1,0:T(2,128)(2,1)} %reshape.115), calls=%async_computation.3 | async-start | bytes 2097152 | tf_op jit(solution)/shard_map/all_to_all | solution.py:141
where the time goes:
time: 603 us; the launch traced here: 598 us
  blocking collectives  242 us (40%)
  starting transfers between devices  175 us (29%)
  local copies, waits for them, and re-layouts  53.3 us (9%)
  waiting for transfers between devices  50 us (8%)
  other arithmetic  43.7 us (7%)
  loops' own time  31 us (5%)
    all_to_all x1, blocking collectives, local(): lax.all_to_all(slot_terms, 'col', split_axis=0, concat_axis=0, tiled=True)  189 us
    all_to_all x1, starting transfers between devices, local(): lax.all_to_all(slot_terms, 'col', split_axis=0, concat_axis=0, tiled=True)  164 us
    psum x1, blocking collectives, local(): summed = lax.psum(jnp.stack(totals), ('row', 'col'))  52.2 us
    all_to_all x2, waiting for transfers between devices, local(): lax.all_to_all(outgoing, 'col', split_axis=0, concat_axis=0, tiled=True)  50 us
    add x24, other arithmetic, sweep(): direction = keep_coef[index] * direction + mix_coef[index] * remainder  34.3 us
    another operation x2, loops' own time, run_pairs(): lax.fori_loop(0, mine_count, one_pair, (collected, jnp.zeros((), jnp.floa...  29.8 us
    dynamic_slice x48, local copies, waits for them, and re-layouts, sweep(): direction = keep_coef[index] * direction + mix_coef[index] * remainder  29.4 us
  transfers between devices with their start and end apart: 3, of which 2 were waited for; matrix products, arithmetic and copies ran while one was open for 0% of the time, Pallas kernels for 0%

commit v1 on v0

--- a/solution.py
+++ b/solution.py
@@ -9,6 +9,28 @@
 ROUNDS = 2
 screen_mu = 0.1
 damping = 0.5
+
+
+def cut_along(value, dim, size):
+    before, after = (value.shape[:dim], value.shape[dim + 1 :])
+    return jnp.moveaxis(value.reshape(*before, size, -1, *after), dim, 0)
+
+
+def in_order(pieces, dim):
+    lengths = list(pieces.shape[1:])
+    lengths[dim] *= pieces.shape[0]
+    return jnp.moveaxis(pieces, 0, dim).reshape(lengths)
+
+
+def exchange_directly(array, axis, split_dim, concat_dim):
+    size, index = (lax.axis_size(axis), lax.axis_index(axis))
+    parts = cut_along(array, split_dim, size)
+    outs = [parts[index]]
+    for turn in range(1, size):
+        sent = parts[(index + turn) % size]
+        outs.append(lax.ppermute(sent, axis, [(i, (i + turn) % size) for i in range(size)]))
+    parts = jnp.stack(outs)[(index - jnp.arange(size)) % size]
+    return in_order(parts, concat_dim)
 
 
 def sweep_table(sweeps):
@@ -131,9 +153,7 @@
             boxes_own.reshape(own_count, edge * plane),
             preferred_element_type=jnp.float32,
         ).astype(jnp.bfloat16)
-        arrived = lax.all_to_all(outgoing, "col", split_axis=0, concat_axis=0, tiled=True).reshape(
-            slots, edge, plane
-        )
+        arrived = exchange_directly(outgoing, "col", 0, 0).reshape(slots, edge, plane)
         gathered, energy = run_pairs(
             arrived, slot_of, slot_of, mine, mine_count, group_offsets, tables, slots
         )

time: 603 us -> 670 us (1.11)
  starting transfers between devices: 175 us -> 384 us
  blocking collectives: 242 us -> 46.2 us
  waiting for transfers between devices: 50 us -> 85.7 us
  local copies, waits for them, and re-layouts: 53.3 us -> 69 us
    all_to_all x1 -> x0, blocking collectives: 189 us -> none  [local(): lax.all_to_all(slot_terms, 'col', split_axis=0, concat_axis=0, tiled=True)]
    all_to_all x1 -> x2, starting transfers between devices: 164 us -> 350 us  [local(): lax.all_to_all(slot_terms, 'col', split_axis=0, concat_axis=0, tiled=True)]
    ppermute x0 -> x14, waiting for transfers between devices: none -> 60.5 us  [exchange_directly(): lax.ppermute(sent, axis, [(i, (i + turn) % size) for i in range(size)])]
    all_to_all x2 -> x0, waiting for transfers between devices: 50 us -> none  [local(): lax.all_to_all(outgoing, 'col', split_axis=0, concat_axis=0, tiled=True)]
    ppermute x0 -> x14, starting transfers between devices: none -> 33.7 us  [exchange_directly(): lax.ppermute(sent, axis, [(i, (i + turn) % size) for i in range(size)])]
    all_to_all x1 -> x2, waiting for transfers between devices: 0.01 us -> 25.2 us  [local(): lax.all_to_all(slot_terms, 'col', split_axis=0, concat_axis=0, tiled=True)]
    all_to_all x2 -> x0, starting transfers between devices: 10.9 us -> none  [local(): lax.all_to_all(outgoing, 'col', split_axis=0, concat_axis=0, tiled=True)]
    unnamed x20 -> x40, local copies, waits for them, and re-layouts: 0.84 us -> 8.17 us
  transfers between devices with their start and end apart: 3 -> 16, of which waited for: 2 -> 7; matrix products, arithmetic and copies ran while one was open for 0% -> 1% of each run, Pallas kernels for 0% -> 0%
where the time goes in v1:
time: 670 us; the launch traced here: 665 us
  starting transfers between devices  384 us (57%)
  waiting for transfers between devices  85.7 us (13%)
  local copies, waits for them, and re-layouts  69 us (10%)
  blocking collectives  46.2 us (7%)
  other arithmetic  44.6 us (7%)
  loops' own time  32.2 us (5%)
    all_to_all x2, starting transfers between devices, local(): lax.all_to_all(slot_terms, 'col', split_axis=0, concat_axis=0, tiled=True)  350 us
    ppermute x14, waiting for transfers between devices, exchange_directly(): lax.ppermute(sent, axis, [(i, (i + turn) % size) for i in range(size)])  60.5 us
    psum x1, blocking collectives, local(): summed = lax.psum(jnp.stack(totals), ('row', 'col'))  46.2 us
    add x24, other arithmetic, sweep(): direction = keep_coef[index] * direction + mix_coef[index] * remainder  35.1 us
    ppermute x14, starting transfers between devices, exchange_directly(): lax.ppermute(sent, axis, [(i, (i + turn) % size) for i in range(size)])  33.7 us
    another operation x2, loops' own time, run_pairs(): lax.fori_loop(0, mine_count, one_pair, (collected, jnp.zeros((), jnp.floa...  31 us
    dynamic_slice x48, local copies, waits for them, and re-layouts, sweep(): direction = keep_coef[index] * direction + mix_coef[index] * remainder  29.9 us
    all_to_all x2, waiting for transfers between devices, local(): lax.all_to_all(slot_terms, 'col', split_axis=0, concat_axis=0, tiled=True)  25.2 us
  transfers between devices with their start and end apart: 16, of which 7 were waited for; matrix products, arithmetic and copies ran while one was open for 1% of the time, Pallas kernels for 0%

profile of v1, /device:TPU:0, one launch (start us, length us, event | category | flops | bytes accessed | tf_op | source)
XLA Modules:
  0.0 664.9 jit_solution(10094902101441193077)
XLA Ops:
  4.8 2.6 constant_dynamic-slice_fusion.17
  7.4 6.1 collective-permute-start.6
  13.9 3.0 collective-permute-start.3
  20.1 17.1 %collective-permute-done = bf16[1,2,32768]{2,0,1:T(2,128)(2,1)} collective-permute-done((bf16[1,2,32768]{2,0,1:T(2,128)(2,1)S(1)}, bf16[1,2,32768]{2,0,1:T(2,128)(2,1)}, u32[]{:S(2)}, u32[]{:S(2)}) %collective-permute-start) | collective-permute-done | bytes 131104 | tf_op jit(solution)/shard_map/ppermute | solution.py:31
  40.1 5.9 collective-permute-done.1
  46.0 5.5 collective-permute-start.2
  51.7 5.4 collective-permute-done.2
  61.1 2.7 gather_fusion
  65.7 55.5 %while.91 = (s32[]{:T(128)}, f32[16,32,1024]{2,1,0:T(8,128)S(1)}, f32[]{:T(128)}, s32[]{:T(128)}, s32[4,2]{0,1:T(2,128)S(1)}, /*index=5*/s32[32]{0:T(128)S(1)}, ...) while((s32[]{:T(128)}, f32[16,32,1024]{2,1,0:T(8,128)S(1)}, ...), condition=%wide.region_6.7_spmd.clone, body=%wide.region_2.6_spmd.sunk.clone.sunk | while | flops 761891 | bytes 5591096 | solution.py:112
  84.1 35.0 %while.94 = (s32[]{:T(128)}, f32[32,1024]{1,0:T(8,128)S(1)}, f32[32,1024]{1,0:T(8,128)S(1)}, f32[32,1024]{1,0:T(8,128)S(1)}, s32[]{:T(128)}, /*index=5*/f32[12]{0:T(128)S(1)}, f32[12]{0:T(128)S(1)}, s32[]{:T(128)}) while((s32[]{:T(128)}, f32[32,1024]{1,0:T(8,128)S(1)}, f32[32,1024]{1,0:T(8,128)S(1)}, ...), condition=%wide.region_4.4_spmd.clone.clone, body=%wide.region_3.3_spmd.sunk.clone.clone.sunk | while | flops 499715 | bytes 3100039 | solution.py:78
  122.9 173.0 %all-to-all-start = ((bf16[8,2,32768]{2,1,0:T(2,128)(2,1)}), bf16[8,2,32768]{2,1,0:T(2,128)(2,1)S(1)}, u32[]{:S(2)}, u32[]{:S(2)}) async-start(bf16[8,2,32768]{2,1,0:T(2,128)(2,1)} %reshape.185), calls=%async_computation | async-start | bytes 2097152 | tf_op jit(solution)/shard_map/all_to_all | solution.py:161
  295.9 25.2 %all-to-all-done = bf16[8,2,32768]{2,1,0:T(2,128)(2,1)S(1)} async-done(((bf16[8,2,32768]{2,1,0:T(2,128)(2,1)}), bf16[8,2,32768]{2,1,0:T(2,128)(2,1)S(1)}, u32[]{:S(2)}, u32[]{:S(2)}) %all-to-all-start) | async-done | bytes 1048608 | tf_op jit(solution)/shard_map/all_to_all | solution.py:161
  323.7 2.6 constant_dynamic-slice_fusion.8
  326.3 2.9 collective-permute-start.13
  329.2 3.3 collective-permute-start.10
  334.4 18.6 %collective-permute-done.7 = bf16[1,2,32768]{2,0,1:T(2,128)(2,1)S(1)} collective-permute-done((bf16[1,2,32768]{2,0,1:T(2,128)(2,1)S(1)}, bf16[1,2,32768]{2,0,1:T(2,128)(2,1)S(1)}, u32[]{:S(2)}, u32[]{:S(2)}) %collective-permute-start.7) | collective-permute-done | bytes 131104 | tf_op jit(solution)/shard_map/ppermute | solution.py:31
  355.8 7.8 %collective-permute-done.8 = bf16[1,2,32768]{2,0,1:T(2,128)(2,1)S(1)} collective-permute-done((bf16[1,2,32768]{2,0,1:T(2,128)(2,1)S(1)}, bf16[1,2,32768]{2,0,1:T(2,128)(2,1)S(1)}, u32[]{:S(2)}, u32[]{:S(2)}) %collective-permute-start.8) | collective-permute-done | bytes 131104 | tf_op jit(solution)/shard_map/ppermute | solution.py:31
  363.6 5.0 collective-permute-start.9
  368.8 5.6 collective-permute-done.9
  375.6 2.8 gather_fusion.1
  380.2 56.9 %while.93 = (s32[]{:T(128)}, f32[16,32,1024]{2,1,0:T(8,128)S(1)}, f32[]{:T(128)}, s32[]{:T(128)}, s32[4,2]{0,1:T(2,128)S(1)}, /*index=5*/s32[32]{0:T(128)S(1)}, ...) while((s32[]{:T(128)}, f32[16,32,1024]{2,1,0:T(8,128)S(1)}, ...), condition=%wide.region_11.12_spmd.clone, body=%wide.region_7.11_spmd.sunk.clone.sunk | while | flops 761891 | bytes 5591080 | solution.py:112
  399.0 36.1 %while.95 = (s32[]{:T(128)}, f32[32,1024]{1,0:T(8,128)S(1)}, f32[32,1024]{1,0:T(8,128)S(1)}, f32[32,1024]{1,0:T(8,128)S(1)}, s32[]{:T(128)}, /*index=5*/f32[12]{0:T(128)S(1)}, f32[12]{0:T(128)S(1)}, s32[]{:T(128)}) while((s32[]{:T(128)}, f32[32,1024]{1,0:T(8,128)S(1)}, f32[32,1024]{1,0:T(8,128)S(1)}, ...), condition=%wide.region_9.9_spmd.clone.clone, body=%wide.region_8.8_spmd.sunk.clone.clone.sunk | while | flops 499715 | bytes 3100039 | solution.py:78
  438.9 177.0 %all-to-all-start.1 = ((bf16[8,2,32768]{2,1,0:T(2,128)(2,1)}), bf16[8,2,32768]{2,1,0:T(2,128)(2,1)S(1)}, u32[]{:S(2)}, u32[]{:S(2)}) async-start(bf16[8,2,32768]{2,1,0:T(2,128)(2,1)} %reshape.188), calls=%async_computation.1 | async-start | bytes 2097152 | tf_op jit(solution)/shard_map/all_to_all | solution.py:161
  616.0 46.2 %psum.7 = f32[2]{0:T(128)S(1)} all-reduce(f32[2]{0:T(128)S(1)} %pad_maximum_fusion), channel_id=1, replica_groups=mesh['row'=4,'col'=8] {'row','col'}, use_global_device_ids=true, to_apply=%region_12.13 | all-reduce | flops 2 | bytes 16 | tf_op jit(solution)/shard_map/psum | solution.py:167
  (297 shorter events, 113.3 us)
Async XLA Ops:
  0.6 18.1 %copy-start = (s32[128,3]{0,1:T(4,128)S(1)}, s32[128,3]{0,1:T(4,128)}, u32[]{:S(2)}) copy-start(s32[128,3]{0,1:T(4,128)} %param.17) | copy-start | bytes 4612
  7.4 53.5 %collective-permute-start.6 = (bf16[1,2,32768]{2,0,1:T(2,128)(2,1)S(1)}, bf16[1,2,32768]{2,0,1:T(2,128)(2,1)S(1)}, u32[]{:S(2)}, u32[]{:S(2)}) collective-permute-start(bf16[1,2,32768]{2,0,1:T(2,128)(2,1)S(1)} %get-tuple-element.840), channel_id=1, source_target_pairs={{0,7},{1,0},{2,1},{3,2},{4,3},{5,4},{6,5},{7,6},{8,15},{9,8},{10,9... | collective-permute-start | bytes 393224 | tf_op jit(solution)/shard_map/ppermute | solution.py:31
  13.5 46.2 %collective-permute-start.5 = (bf16[1,2,32768]{2,0,1:T(2,128)(2,1)S(1)}, bf16[1,2,32768]{2,0,1:T(2,128)(2,1)}, u32[]{:S(2)}, u32[]{:S(2)}) collective-permute-start(bf16[1,2,32768]{2,0,1:T(2,128)(2,1)S(1)} %get-tuple-element.841), channel_id=1, source_target_pairs={{0,6},{1,7},{2,0},{3,1},{4,2},{5,3},{6,4},{7,5},{8,14},{9,15},{10,... | collective-permute-start | bytes 393224 | tf_op jit(solution)/shard_map/ppermute | solution.py:31
  13.9 44.6 %collective-permute-start.4 = (bf16[1,2,32768]{2,0,1:T(2,128)(2,1)S(1)}, bf16[1,2,32768]{2,0,1:T(2,128)(2,1)}, u32[]{:S(2)}, u32[]{:S(2)}) collective-permute-start(bf16[1,2,32768]{2,0,1:T(2,128)(2,1)S(1)} %get-tuple-element.842), channel_id=1, source_target_pairs={{0,5},{1,6},{2,7},{3,0},{4,1},{5,2},{6,3},{7,4},{8,13},{9,14},{10,... | collective-permute-start | bytes 393224 | tf_op jit(solution)/shard_map/ppermute | solution.py:31
  13.9 43.4 %collective-permute-start.3 = (bf16[1,2,32768]{2,0,1:T(2,128)(2,1)S(1)}, bf16[1,2,32768]{2,0,1:T(2,128)(2,1)}, u32[]{:S(2)}, u32[]{:S(2)}) collective-permute-start(bf16[1,2,32768]{2,0,1:T(2,128)(2,1)S(1)} %get-tuple-element.843), channel_id=1, source_target_pairs={{0,4},{1,5},{2,6},{3,7},{4,0},{5,1},{6,2},{7,3},{8,12},{9,13},{10,... | collective-permute-start | bytes 393224 | tf_op jit(solution)/shard_map/ppermute | solution.py:31
  16.9 20.3 %collective-permute-start = (bf16[1,2,32768]{2,0,1:T(2,128)(2,1)S(1)}, bf16[1,2,32768]{2,0,1:T(2,128)(2,1)}, u32[]{:S(2)}, u32[]{:S(2)}) collective-permute-start(bf16[1,2,32768]{2,0,1:T(2,128)(2,1)S(1)} %get-tuple-element.846), channel_id=1, source_target_pairs={{0,1},{1,2},{2,3},{3,4},{4,5},{5,6},{6,7},{7,0},{8,9},{9,10},{10,1... | collective-permute-start | bytes 393224 | tf_op jit(solution)/shard_map/ppermute | solution.py:31
  20.1 43.7 %copy-start.9 = (s32[1024]{0:T(1024)}, s32[1024]{0:T(1024)S(1)}, u32[]{:S(2)}) copy-start(s32[1024]{0:T(1024)S(1)} %pad_clamp_fusion) | copy-start | bytes 12292
  37.2 8.8 %collective-permute-start.1 = (bf16[1,2,32768]{2,0,1:T(2,128)(2,1)S(1)}, bf16[1,2,32768]{2,0,1:T(2,128)(2,1)S(1)}, u32[]{:S(2)}, u32[]{:S(2)}) collective-permute-start(bf16[1,2,32768]{2,0,1:T(2,128)(2,1)S(1)} %get-tuple-element.845), channel_id=1, source_target_pairs={{0,2},{1,3},{2,4},{3,5},{4,6},{5,7},{6,0},{7,1},{8,10},{9,11},{10,... | collective-permute-start | bytes 393224 | tf_op jit(solution)/shard_map/ppermute | solution.py:31
  46.0 11.2 %collective-permute-start.2 = (bf16[1,2,32768]{2,0,1:T(2,128)(2,1)S(1)}, bf16[1,2,32768]{2,0,1:T(2,128)(2,1)S(1)}, u32[]{:S(2)}, u32[]{:S(2)}) collective-permute-start(bf16[1,2,32768]{2,0,1:T(2,128)(2,1)S(1)} %get-tuple-element.844), channel_id=1, source_target_pairs={{0,3},{1,4},{2,5},{3,6},{4,7},{5,0},{6,1},{7,2},{8,11},{9,12},{10,... | collective-permute-start | bytes 393224 | tf_op jit(solution)/shard_map/ppermute | solution.py:31
  121.3 199.7 %copy-start.8 = (pred[8,2,4]{0,2,1:T(4,128)(4,1)S(1)}, pred[8,2,4]{0,2,1:T(4,128)(4,1)}, u32[]{:S(2)}) copy-start(pred[8,2,4]{0,2,1:T(4,128)(4,1)} %copy-done.7) | copy-start | bytes 196
  122.9 199.7 %copy-start.1 = (f32[4,32,1024]{2,1,0:T(8,128)S(1)}, f32[4,32,1024]{2,1,0:T(8,128)}, u32[]{:S(2)}) copy-start(f32[4,32,1024]{2,1,0:T(8,128)} %param.15) | copy-start | bytes 1572868
  122.9 199.7 %copy-start.5 = (f32[4,32,1024]{2,1,0:T(8,128)S(1)}, f32[4,32,1024]{2,1,0:T(8,128)}, u32[]{:S(2)}) copy-start(f32[4,32,1024]{2,1,0:T(8,128)} %param.16) | copy-start | bytes 1572868
  122.9 198.1 %all-to-all-start = ((bf16[8,2,32768]{2,1,0:T(2,128)(2,1)}), bf16[8,2,32768]{2,1,0:T(2,128)(2,1)S(1)}, u32[]{:S(2)}, u32[]{:S(2)}) async-start(bf16[8,2,32768]{2,1,0:T(2,128)(2,1)} %reshape.185), calls=%async_computation | async-start | bytes 2097152 | tf_op jit(solution)/shard_map/all_to_all | solution.py:161
  326.3 49.0 %collective-permute-start.13 = (bf16[1,2,32768]{2,0,1:T(2,128)(2,1)S(1)}, bf16[1,2,32768]{2,0,1:T(2,128)(2,1)S(1)}, u32[]{:S(2)}, u32[]{:S(2)}) collective-permute-start(bf16[1,2,32768]{2,0,1:T(2,128)(2,1)S(1)} %get-tuple-element.832), channel_id=1, source_target_pairs={{0,7},{1,0},{2,1},{3,2},{4,3},{5,4},{6,5},{7,6},{8,15},{9,8},{10,9... | collective-permute-start | bytes 393224 | tf_op jit(solution)/shard_map/ppermute | solution.py:31
  329.2 45.9 %collective-permute-start.12 = (bf16[1,2,32768]{2,0,1:T(2,128)(2,1)S(1)}, bf16[1,2,32768]{2,0,1:T(2,128)(2,1)S(1)}, u32[]{:S(2)}, u32[]{:S(2)}) collective-permute-start(bf16[1,2,32768]{2,0,1:T(2,128)(2,1)S(1)} %get-tuple-element.833), channel_id=1, source_target_pairs={{0,6},{1,7},{2,0},{3,1},{4,2},{5,3},{6,4},{7,5},{8,14},{9,15},{10,... | collective-permute-start | bytes 393224 | tf_op jit(solution)/shard_map/ppermute | solution.py:31
  329.2 45.7 %collective-permute-start.11 = (bf16[1,2,32768]{2,0,1:T(2,128)(2,1)S(1)}, bf16[1,2,32768]{2,0,1:T(2,128)(2,1)S(1)}, u32[]{:S(2)}, u32[]{:S(2)}) collective-permute-start(bf16[1,2,32768]{2,0,1:T(2,128)(2,1)S(1)} %get-tuple-element.834), channel_id=1, source_target_pairs={{0,5},{1,6},{2,7},{3,0},{4,1},{5,2},{6,3},{7,4},{8,13},{9,14},{10,... | collective-permute-start | bytes 393224 | tf_op jit(solution)/shard_map/ppermute | solution.py:31
  329.2 45.4 %collective-permute-start.10 = (bf16[1,2,32768]{2,0,1:T(2,128)(2,1)S(1)}, bf16[1,2,32768]{2,0,1:T(2,128)(2,1)S(1)}, u32[]{:S(2)}, u32[]{:S(2)}) collective-permute-start(bf16[1,2,32768]{2,0,1:T(2,128)(2,1)S(1)} %get-tuple-element.835), channel_id=1, source_target_pairs={{0,4},{1,5},{2,6},{3,7},{4,0},{5,1},{6,2},{7,3},{8,12},{9,13},{10,... | collective-permute-start | bytes 393224 | tf_op jit(solution)/shard_map/ppermute | solution.py:31
  332.5 20.5 %collective-permute-start.7 = (bf16[1,2,32768]{2,0,1:T(2,128)(2,1)S(1)}, bf16[1,2,32768]{2,0,1:T(2,128)(2,1)S(1)}, u32[]{:S(2)}, u32[]{:S(2)}) collective-permute-start(bf16[1,2,32768]{2,0,1:T(2,128)(2,1)S(1)} %get-tuple-element.838), channel_id=1, source_target_pairs={{0,1},{1,2},{2,3},{3,4},{4,5},{5,6},{6,7},{7,0},{8,9},{9,10},{10,1... | collective-permute-start | bytes 393224 | tf_op jit(solution)/shard_map/ppermute | solution.py:31
  353.0 10.6 %collective-permute-start.8 = (bf16[1,2,32768]{2,0,1:T(2,128)(2,1)S(1)}, bf16[1,2,32768]{2,0,1:T(2,128)(2,1)S(1)}, u32[]{:S(2)}, u32[]{:S(2)}) collective-permute-start(bf16[1,2,32768]{2,0,1:T(2,128)(2,1)S(1)} %get-tuple-element.837), channel_id=1, source_target_pairs={{0,2},{1,3},{2,4},{3,5},{4,6},{5,7},{6,0},{7,1},{8,10},{9,11},{10,... | collective-permute-start | bytes 393224 | tf_op jit(solution)/shard_map/ppermute | solution.py:31
  363.6 10.8 %collective-permute-start.9 = (bf16[1,2,32768]{2,0,1:T(2,128)(2,1)S(1)}, bf16[1,2,32768]{2,0,1:T(2,128)(2,1)S(1)}, u32[]{:S(2)}, u32[]{:S(2)}) collective-permute-start(bf16[1,2,32768]{2,0,1:T(2,128)(2,1)S(1)} %get-tuple-element.836), channel_id=1, source_target_pairs={{0,3},{1,4},{2,5},{3,6},{4,7},{5,0},{6,1},{7,2},{8,11},{9,12},{10,... | collective-permute-start | bytes 393224 | tf_op jit(solution)/shard_map/ppermute | solution.py:31
  438.9 224.5 %copy-start.2 = (f32[4,32,1024]{2,1,0:T(8,128)S(1)}, f32[4,32,1024]{2,1,0:T(8,128)}, u32[]{:S(2)}) copy-start(f32[4,32,1024]{2,1,0:T(8,128)} %param.15) | copy-start | bytes 1572868
  438.9 224.5 %copy-start.4 = (f32[4,32768,1]{1,0,2:T(4,128)S(1)}, f32[4,32768,1]{1,0,2:T(4,128)}, u32[]{:S(2)}) copy-start(f32[4,32768,1]{1,0,2:T(4,128)} %copy-done.3) | copy-start | bytes 1572868
  438.9 224.5 %copy-start.6 = (f32[4,32,1024]{2,1,0:T(8,128)S(1)}, f32[4,32,1024]{2,1,0:T(8,128)}, u32[]{:S(2)}) copy-start(f32[4,32,1024]{2,1,0:T(8,128)} %param.16) | copy-start | bytes 1572868
  438.9 223.8 %all-to-all-start.1 = ((bf16[8,2,32768]{2,1,0:T(2,128)(2,1)}), bf16[8,2,32768]{2,1,0:T(2,128)(2,1)S(1)}, u32[]{:S(2)}, u32[]{:S(2)}) async-start(bf16[8,2,32768]{2,1,0:T(2,128)(2,1)} %reshape.188), calls=%async_computation.1 | async-start | bytes 2097152 | tf_op jit(solution)/shard_map/all_to_all | solution.py:161
  (5 other events, 19.2 us)
